TPU v7x, 32 devices: a whole 2x2x4 slice. The times are simulated.
32 devices in a mesh: row: 2 (over x), col: 8 (over z, core), depth: 2 (over y).
Axes of the slice: x: 2, y: 2, z: 4, core: 2. Of those that a mesh axis runs over, the one named last changes fastest.
Arguments:
- pair_blocks: bfloat16 [416, 128, 128], P(('row', 'col', 'depth')), may hold values from -0.375 to 0.375
- dest_owner: int32 [416, 1], P(('row', 'col', 'depth')), may hold values from 0 to 7; in each aligned block of 13 rows (0 to 12, 13 to 25, ...) at most 2 rows name the same one
- dest_tile: int32 [416], P(('row', 'col', 'depth')), may hold values from 0 to 63
- chemical_potential: float32 [1], replicated, may hold values from 0.2 to 0.8
Outputs:
- sign_step: float32 [4096, 4096], P('row', 'col')
Inputs may be any that keep to these rules, and one draw needn't show every extreme that they name: `dest_owner`: among the 13 pair blocks of one device, no destination col index appears more than 2 times, a bound that some block reaches.
All inputs are finite; a program needn't handle non-finite values.
Results may differ from a plain program's by a relative error of at most 0.0038.
Values may be sent and summed in bfloat16 or wider, within the bound.
A program may use at most 64 MiB of HBM per device.

v0:
```python
import jax
import jax.numpy as jnp
from jax import lax
from jax.sharding import PartitionSpec as P

TC = 4
CAP = 2


def assemble(received, labels, tile_count):
    one_hot = (
        labels.astype(jnp.float32)[None, :] == jnp.arange(tile_count, dtype=jnp.float32)[:, None]
    ).astype(jnp.bfloat16)
    return jnp.dot(one_hot, received, preferred_element_type=jnp.float32)


def product(left_matrix, right_matrix):
    layer_count = lax.axis_size("depth")
    layer_index = lax.axis_index("depth")
    rows_local, cols_local = left_matrix.shape
    half_rows = rows_local // layer_count
    own_part = lax.dynamic_slice_in_dim(left_matrix, layer_index * half_rows, half_rows, 0)
    row_panel = lax.all_gather(right_matrix, "row", axis=0, tiled=True)
    partial_rows = jnp.dot(
        lax.all_gather(own_part, "col", axis=1, tiled=True),
        row_panel,
        preferred_element_type=jnp.float32,
    )
    return lax.all_gather(partial_rows, "depth", axis=0, tiled=True)


def shards(pair_blocks, dest_owner, dest_tile, chemical_potential):
    col_count = lax.axis_size("col")
    row_count = lax.axis_size("row")
    block_count = pair_blocks.shape[0]
    tile_size = pair_blocks.shape[1]
    tile_rows = TC * col_count // row_count
    tile_count = tile_rows * TC
    flat_blocks = pair_blocks.reshape(block_count, tile_size * tile_size)
    owners = dest_owner[:, 0]
    owner_hot = (owners[:, None] == jnp.arange(col_count, dtype=jnp.int32)[None, :]).astype(
        jnp.int32
    )
    earlier = jnp.cumsum(owner_hot, axis=0) - owner_hot
    slot_rank = jnp.sum(earlier * owner_hot, axis=1)
    slot_index = owners * CAP + slot_rank
    picker = (slot_index[None, :] == jnp.arange(col_count * CAP, dtype=jnp.int32)[:, None]).astype(
        jnp.int32
    )
    send_blocks = jnp.dot(
        picker.astype(jnp.bfloat16), flat_blocks, preferred_element_type=jnp.float32
    ).astype(jnp.bfloat16)
    send_blocks = send_blocks.reshape(col_count, CAP, tile_size * tile_size)
    send_labels = (
        (jnp.sum(picker * (dest_tile[None, :] + 1), axis=1) - 1)
        .astype(jnp.float32)
        .astype(jnp.bfloat16)
    )
    send_labels = send_labels.reshape(col_count, CAP)
    got_blocks, got_labels = (
        lax.all_to_all(send_blocks, "col", split_axis=0, concat_axis=0, tiled=True),
        lax.all_to_all(send_labels, "col", split_axis=0, concat_axis=0, tiled=True),
    )
    own_tiles = assemble(
        got_blocks.reshape(-1, tile_size * tile_size), got_labels.reshape(-1), tile_count
    )
    assembled = lax.psum(own_tiles, "depth")
    hamiltonian = assembled.reshape(tile_rows, TC, tile_size, tile_size).transpose(0, 2, 1, 3)
    hamiltonian = hamiltonian.reshape(tile_rows * tile_size, TC * tile_size)
    rows_local, cols_local = hamiltonian.shape
    row_first = lax.axis_index("row") * rows_local
    col_first = lax.axis_index("col") * cols_local
    identity = (
        (row_first + jnp.arange(rows_local, dtype=jnp.int32))[:, None]
        == (col_first + jnp.arange(cols_local, dtype=jnp.int32))[None, :]
    ).astype(jnp.float32)
    left_matrix = (hamiltonian - chemical_potential[0] * identity).astype(jnp.bfloat16)
    squared = product(left_matrix, left_matrix)
    right_matrix = (3.0 * identity - squared).astype(jnp.bfloat16)
    return 0.5 * product(left_matrix, right_matrix)


def solution(mesh):
    in_specs = (
        P(("row", "col", "depth"), None, None),
        P(("row", "col", "depth"), None),
        P(("row", "col", "depth")),
        P(),
    )
    out_specs = P("row", "col")
    return jax.shard_map(shards, mesh=mesh, in_specs=in_specs, out_specs=out_specs, check_vma=False)
```

profile of v0, /device:TPU:1, one launch (start us, length us, event | category | flops | bytes accessed | tf_op | source)
XLA Modules:
  0.0 516.5 jit_solution(18420871151592003025)
XLA Ops:
  6.5 0.7 fusion.6
  7.2 0.2 reduce_window_sum.11
  7.4 0.7 select_reduce_fusion.1
  8.0 0.7 multiply_add_fusion
  8.8 0.7 convert_element_type.68
  9.5 6.4 %all-to-all-start = ((bf16[8,1,2]{2,1,0:T(2,128)(2,1)}), bf16[8,1,2]{2,1,0:T(2,128)(2,1)S(1)}, u32[]{:S(2)}, u32[]{:S(2)}) async-start(bf16[8,1,2]{2,1,0:T(2,128)(2,1)} %convert_element_type.68), calls=%async_computation | async-start | bytes 8192 | tf_op jit(solution)/shard_map/all_to_all | solution.py:62
  15.9 1.1 pad
  17.0 0.3 copy.12
  17.3 0.3 convolution_convert_fusion
  17.6 1.1 reshape.67
  18.7 2.0 all-to-all-done
  20.8 4.1 all-to-all-start.1
  25.0 14.4 %all-to-all-done.1 = bf16[8,2,16384]{2,1,0:T(2,128)(2,1)S(1)} async-done(((bf16[8,2,16384]{2,1,0:T(2,128)(2,1)}), bf16[8,2,16384]{2,1,0:T(2,128)(2,1)S(1)}, u32[]{:S(2)}, u32[]{:S(2)}) %all-to-all-start.1) | async-done | bytes 524320 | tf_op jit(solution)/shard_map/all_to_all | solution.py:61
  39.4 0.2 reshape.68
  39.6 0.7 convolution_bitcast_fusion
  40.3 2.8 copy.13
  43.0 5.5 %copy.10 = f32[16,4,128,128]{2,0,3,1:T(8,128)} copy(f32[16,4,128,128]{3,2,1,0:T(8,128)} %bitcast.25) | data formatting | bytes 8388608 | tf_op jit(solution)/shard_map/reshape | solution.py:68
  48.5 6.2 %copy.16 = f32[64,8,16,128]{3,1,2,0:T(8,128)} copy(f32[64,8,16,128]{3,2,1,0:T(8,128)} %bitcast.26) | data formatting | bytes 8388608
  54.6 5.4 %copy.11 = f32[2048,512]{1,0:T(8,128)} copy(f32[2048,512]{0,1:T(8,128)} %bitcast.27) | data formatting | bytes 8388608 | tf_op jit(solution)/shard_map/reshape | solution.py:69
  60.8 106.4 %all-reduce.2.cloned.1.call-done = f32[2048,512]{1,0:T(8,128)} async-done(((f32[2048,512]{1,0:T(8,128)}), f32[2048,512]{1,0:T(8,128)}) %all-reduce.2.cloned.1.call-update) | async-done | bytes 4194320 | tf_op jit(solution)/shard_map/psum | solution.py:67
  167.2 3.5 fusion.1
  170.7 2.3 constant_dynamic-slice_fusion
  173.1 54.4 %all-gather.8.cloned.1.call-done = bf16[4096,512]{1,0:T(8,128)(2,1)} async-done(((bf16[2048,512]{1,0:T(8,128)(2,1)}), bf16[4096,512]{1,0:T(8,128)(2,1)}) %all-gather.8.cloned.1.call-update) | async-done | bytes 4194320 | tf_op jit(solution)/shard_map/all_gather | solution.py:23
  227.6 84.2 %all-gather.6.cloned.1.call-done = bf16[1024,4096]{1,0:T(8,128)(2,1)} async-done(((bf16[1024,512]{1,0:T(8,128)(2,1)}), bf16[1024,4096]{1,0:T(8,128)(2,1)}) %all-gather.6.cloned.1.call-update) | async-done | bytes 8388624 | tf_op jit(solution)/shard_map/all_gather | solution.py:25
  311.8 10.4 %fusion.7 = f32[1024,512]{1,0:T(8,128)} fusion(bf16[1024,4096]{1,0:T(8,128)(2,1)} %all-gather.6.cloned.1.call-done, bf16[4096,512]{1,0:T(8,128)(2,1)} %all-gather.8.cloned.1.call-done), kind=kOutput, calls=%fused_computation.26 | convolution fusion | flops 4294967296 | bytes 14680064 | tf_op jit(solution)/shard_map/dot_general | solution.py:24
  322.2 55.0 %all-gather.10.cloned.1.call-done = f32[2048,512]{1,0:T(8,128)} async-done(((f32[1024,512]{1,0:T(8,128)}), f32[2048,512]{1,0:T(8,128)}) %all-gather.10.cloned.1.call-update) | async-done | bytes 4194320 | tf_op jit(solution)/shard_map/all_gather | solution.py:29
  377.2 3.5 fusion.3
  380.7 0.2 all-gather.14.cloned.1.call-start
  381.0 56.7 %all-gather.12.cloned.1.call-done = bf16[4096,512]{1,0:T(8,128)(2,1)} async-done(((bf16[2048,512]{1,0:T(8,128)(2,1)}), bf16[4096,512]{1,0:T(8,128)(2,1)}) %all-gather.12.cloned.1.call-update) | async-done | bytes 4194320 | tf_op jit(solution)/shard_map/all_gather | solution.py:23
  437.6 10.4 %fusion.8 = f32[1024,512]{1,0:T(8,128)} fusion(bf16[1024,4096]{1,0:T(8,128)(2,1)} %all-gather.6.cloned.1.call-done, bf16[4096,512]{1,0:T(8,128)(2,1)} %all-gather.12.cloned.1.call-done), kind=kOutput, calls=%fused_computation.27 | convolution fusion | flops 4294967296 | bytes 14680064 | tf_op jit(solution)/shard_map/dot_general | solution.py:24
  448.0 56.9 %all-gather.14.cloned.1.call-done = f32[2048,512]{1,0:T(8,128)} async-done(((f32[1024,512]{1,0:T(8,128)}), f32[2048,512]{1,0:T(8,128)}) %all-gather.14.cloned.1.call-update) | async-done | bytes 4194320 | tf_op jit(solution)/shard_map/all_gather | solution.py:29
  504.9 4.7 broadcast_multiply_fusion
  (17 shorter events, 0.5 us)
Async XLA Ops:
  9.5 11.2 %all-to-all-start = ((bf16[8,1,2]{2,1,0:T(2,128)(2,1)}), bf16[8,1,2]{2,1,0:T(2,128)(2,1)S(1)}, u32[]{:S(2)}, u32[]{:S(2)}) async-start(bf16[8,1,2]{2,1,0:T(2,128)(2,1)} %convert_element_type.68), calls=%async_computation | async-start | bytes 8192 | tf_op jit(solution)/shard_map/all_to_all | solution.py:62
  20.8 18.6 %all-to-all-start.1 = ((bf16[8,2,16384]{2,1,0:T(2,128)(2,1)}), bf16[8,2,16384]{2,1,0:T(2,128)(2,1)S(1)}, u32[]{:S(2)}, u32[]{:S(2)}) async-start(bf16[8,2,16384]{2,1,0:T(2,128)(2,1)} %reshape.67), calls=%async_computation.1 | async-start | bytes 1048576 | tf_op jit(solution)/shard_map/all_to_all | solution.py:61
  24.9 142.3 %all-reduce.2.cloned.1.call-start = ((), (), s32[]{:S(2)}) async-start(), calls=%async_computation.2 | async-start | bytes 8388608 | tf_op jit(solution)/shard_map/psum | solution.py:67
  60.0 167.6 %all-gather.8.cloned.1.call-start = ((), (), s32[]{:S(2)}) async-start(), calls=%async_computation.4 | async-start | bytes 6291456 | tf_op jit(solution)/shard_map/all_gather | solution.py:23
  170.7 141.1 %all-gather.6.cloned.1.call-start = ((), (), s32[]{:S(2)}) async-start(), calls=%async_computation.3 | async-start | bytes 9437184 | tf_op jit(solution)/shard_map/all_gather | solution.py:25
  173.1 204.1 %all-gather.10.cloned.1.call-start = ((), (), s32[]{:S(2)}) async-start(), calls=%async_computation.5 | async-start | bytes 6291456 | tf_op jit(solution)/shard_map/all_gather | solution.py:29
  322.2 115.4 %all-gather.12.cloned.1.call-start = ((), (), s32[]{:S(2)}) async-start(), calls=%async_computation.6 | async-start | bytes 6291456 | tf_op jit(solution)/shard_map/all_gather | solution.py:23
  380.7 124.2 %all-gather.14.cloned.1.call-start = ((), (), s32[]{:S(2)}) async-start(), calls=%async_computation.7 | async-start | bytes 6291456 | tf_op jit(solution)/shard_map/all_gather | solution.py:29
Sparse Core Ops, SparseCore 0:
  60.1 106.9 all-reduce.1
  170.8 56.7 all-gather.7
  229.3 82.4 all-gather.5
  322.3 54.8 all-gather.9
  380.9 56.7 all-gather.11
  448.2 56.7 all-gather.13
where the time goes:
time: 518 us; the launch traced here: 516 us
  waiting for transfers between devices  430 us (83%)
  local copies, waits for them, and re-layouts  25.6 us (5%)
  matrix products  21.7 us (4%)
  between operations  14.2 us (3%)
  other arithmetic  14 us (3%)
  starting transfers between devices  10.9 us (2%)
    all_gather x2, waiting for transfers between devices, product(): return lax.all_gather(partial_rows, 'depth', axis=0, tiled=True)  112 us
    all_gather x2, waiting for transfers between devices, product(): row_panel = lax.all_gather(right_matrix, 'row', axis=0, tiled=True)  111 us
    psum x1, waiting for transfers between devices, shards(): assembled = lax.psum(own_tiles, 'depth')  106 us
    all_gather x1, waiting for transfers between devices, product(): lax.all_gather(own_part, 'col', axis=1, tiled=True)  84.2 us
    dot_general x2, matrix products, product(): jnp.dot(lax.all_gather(own_part, 'col', axis=1, tiled=True), row_panel, p...  20.7 us
    all_to_all x1, waiting for transfers between devices, shards(): lax.all_to_all(send_blocks, 'col', split_axis=0, concat_axis=0, tiled=True)  14.4 us
  transfers between devices with their start and end apart: 8, of which 8 were waited for; matrix products, arithmetic and copies ran while one was open for 1% of the time, Pallas kernels for 0%

commit v1 on v0

--- a/solution.py
+++ b/solution.py
@@ -1,10 +1,16 @@
+import functools
+
 import jax
 import jax.numpy as jnp
 from jax import lax
+from jax.experimental import pallas as pl
+from jax.experimental.pallas import tpu as pltpu
 from jax.sharding import PartitionSpec as P
 
 TC = 4
 CAP = 2
+TILE = 128
+LABEL_ROWS = 16
 
 
 def assemble(received, labels, tile_count):
@@ -80,6 +86,263 @@
     return 0.5 * product(left_matrix, right_matrix)
 
 
+def gather_kernel(z_count, split, own_ref, all_ref, local_sem, send_sem, recv_sem):
+    x = lax.axis_index("row")
+    y = lax.axis_index("depth")
+    c = lax.axis_index("col")
+    z, q = c // 2, c % 2
+    rows = own_ref.shape[0]
+    spans = ((0, split), (split, rows - split))
+
+    def device(px, py, pz, pq):
+        return {"row": px, "col": pz * 2 + pq, "depth": py}
+
+    def chip(px, py, pz):
+        return (px * 2 + py) * z_count + pz
+
+    z_others = [lax.rem(z + k, z_count) for k in range(1, z_count)]
+    if z_count == 4:
+        z_others = [z + 1 - 2 * lax.rem(z, 2), lax.rem(z + 2, 4), 3 - z]
+    x_peer = device(1 - x, y, z, q)
+    y_peer = device(x, 1 - y, z, q)
+    sibling = device(x, y, z, 1 - q)
+    peers = [device(x, y, pz, q) for pz in z_others] + [x_peer, y_peer, sibling]
+
+    barrier = pltpu.get_barrier_semaphore()
+    for peer in peers:
+        pl.semaphore_signal(barrier, inc=1, device_id=peer, device_id_type=pl.DeviceIdType.MESH)
+    pl.semaphore_wait(barrier, len(peers))
+
+    started = []
+    sends = [0]
+
+    def place(source, part, parity):
+        px, py, pz = source
+        first, size = spans[part]
+        return all_ref.at[px * (z_count * 4) + (pz * 2 + parity) * 2 + py, pl.ds(first, size)]
+
+    def send(source, part, peer, own, to_sibling=0):
+        first, size = spans[part]
+        copy = pltpu.make_async_remote_copy(
+            src_ref=own_ref.at[pl.ds(first, size)] if own else place(source, part, q),
+            dst_ref=place(source, part, q),
+            send_sem=send_sem.at[sends[0]],
+            recv_sem=recv_sem.at[part, to_sibling, chip(*source)],
+            device_id=peer,
+            device_id_type=pl.DeviceIdType.MESH,
+        )
+        sends[0] += 1
+        copy.start()
+        started.append(copy)
+
+    def arrived(source, part, from_sibling=0):
+        parity = 1 - q if from_sibling else q
+        target = place(source, part, parity)
+        pltpu.make_async_remote_copy(
+            src_ref=target,
+            dst_ref=target,
+            send_sem=send_sem.at[0],
+            recv_sem=recv_sem.at[part, from_sibling, chip(*source)],
+            device_id=sibling,
+            device_id_type=pl.DeviceIdType.MESH,
+        ).wait_recv()
+
+    first_peer, last_peer = (x_peer, y_peer), (y_peer, x_peer)
+    own = (x, y, z)
+    for pz in z_others:
+        for part in range(2):
+            send(own, part, device(x, y, pz, q), True)
+    for part in range(2):
+        send(own, part, first_peer[part], True)
+    for part in range(2):
+        send(own, part, last_peer[part], True)
+        send(own, part, sibling, True, 1)
+    keep = pltpu.make_async_copy(
+        own_ref, all_ref.at[x * (z_count * 4) + c * 2 + y], local_sem
+    )
+    keep.start()
+
+    def second(part, pz):
+        return (1 - x, y, pz) if part == 0 else (x, 1 - y, pz)
+
+    def third(part, pz):
+        return ((x, 1 - y, pz), (1 - x, 1 - y, pz)) if part == 0 else (
+            (1 - x, y, pz), (1 - x, 1 - y, pz))
+
+    order = [z] + z_others
+    for step, pz in enumerate(order):
+        for part in range(2):
+            if step:
+                arrived((x, y, pz), part)
+                send((x, y, pz), part, first_peer[part], False)
+                send((x, y, pz), part, last_peer[part], False)
+                send((x, y, pz), part, sibling, False, 1)
+        for part in range(2):
+            source = second(part, pz)
+            arrived(source, part)
+            send(source, part, last_peer[part], False)
+            send(source, part, sibling, False, 1)
+    for pz in order:
+        for part in range(2):
+            for source in third(part, pz):
+                arrived(source, part)
+                send(source, part, sibling, False, 1)
+    for px in range(2):
+        for py in range(2):
+            for pz in range(z_count):
+                for part in range(2):
+                    arrived((px, py, pz), part, 1)
+    for copy in started:
+        copy.wait_send()
+    keep.wait()
+
+
+def gather_pieces(piece, devices):
+    rows, width = piece.shape
+    z_count = lax.axis_size("col") // 2
+    sends = 2 * ((z_count - 1) + 2 + (z_count - 1) * 2 + z_count + 4 * z_count)
+    return pl.pallas_call(
+        functools.partial(gather_kernel, z_count, (rows // 32 + 1) // 1 * 16),
+        out_shape=jax.ShapeDtypeStruct((devices, rows, width), piece.dtype),
+        in_specs=[pl.BlockSpec(memory_space=pl.ANY)],
+        out_specs=pl.BlockSpec(memory_space=pl.ANY),
+        scratch_shapes=[
+            pltpu.SemaphoreType.DMA(()),
+            pltpu.SemaphoreType.DMA((sends,)),
+            pltpu.SemaphoreType.DMA((2, 2, 4 * z_count)),
+        ],
+        compiler_params=pltpu.CompilerParams(collective_id=0, has_side_effects=True),
+    )(piece)
+
+
+def step_kernel(
+    block_count, chunk, where_ref, next_ref, place_ref, shift_ref, all_ref, out_ref,
+    blocks, left, right, sem
+):
+    devices = all_ref.shape[0]
+    order = left.shape[0]
+    grid_tiles = order // TILE
+    rows_local, cols_local = out_ref.shape
+    shift = shift_ref[0]
+
+    fetch = pltpu.make_async_copy(all_ref.at[:, pl.ds(0, block_count * TILE)], blocks, sem)
+    fetch.start()
+
+    eye = (
+        lax.broadcasted_iota(jnp.int32, (TILE, TILE), 0)
+        == lax.broadcasted_iota(jnp.int32, (TILE, TILE), 1)
+    )
+    shifted = jnp.where(eye, shift, 0.0)
+
+    @pl.loop(0, grid_tiles)
+    def _(i):
+        rows = pl.ds(pl.multiple_of(i * TILE, TILE), TILE)
+        left[rows, :] = jnp.zeros((TILE, order), left.dtype)
+        left[rows, rows] = (-shifted).astype(left.dtype)
+
+    fetch.wait()
+
+    @pl.loop(0, devices)
+    def _(g):
+        for p in range(block_count):
+            b = g * block_count + p
+            tile = where_ref[b]
+            follower = next_ref[b]
+            i = tile // grid_tiles
+            k = tile % grid_tiles
+            plain = jnp.logical_and(follower < 0, i != k)
+            rows = pl.ds(pl.multiple_of(i * TILE, TILE), TILE)
+            cols = pl.ds(pl.multiple_of(k * TILE, TILE), TILE)
+            own = pl.ds(p * TILE, TILE)
+
+            @pl.when(jnp.logical_and(tile >= 0, plain))
+            def _():
+                left[rows, cols] = blocks[g, own, :]
+
+            @pl.when(jnp.logical_and(tile >= 0, jnp.logical_not(plain)))
+            def _():
+                def more(carry):
+                    return carry[0] >= 0
+
+                def add(carry):
+                    n, total = carry
+                    row = pl.multiple_of((n % block_count) * TILE, TILE)
+                    extra = blocks[n // block_count, pl.ds(row, TILE), :]
+                    return next_ref[n], total + extra.astype(jnp.float32)
+
+                _, total = lax.while_loop(
+                    more, add, (follower, blocks[g, own, :].astype(jnp.float32))
+                )
+                left[rows, cols] = (total - jnp.where(i == k, shifted, 0.0)).astype(left.dtype)
+
+    row_first = place_ref[0] * rows_local
+    col_first = pl.multiple_of(place_ref[1] * cols_local, cols_local)
+    columns = pl.ds(col_first, cols_local)
+
+    @pl.loop(0, order // chunk)
+    def _(m):
+        first = pl.multiple_of(m * chunk, chunk)
+        rows = pl.ds(first, chunk)
+        squared = jnp.dot(left[rows, :], left[:, columns], preferred_element_type=jnp.float32)
+        on_diagonal = (
+            first + lax.broadcasted_iota(jnp.int32, (chunk, cols_local), 0)
+            == col_first + lax.broadcasted_iota(jnp.int32, (chunk, cols_local), 1)
+        )
+        right[rows, :] = (jnp.where(on_diagonal, 3.0, 0.0) - squared).astype(right.dtype)
+
+    @pl.loop(0, rows_local // chunk)
+    def _(m):
+        first = pl.multiple_of(m * chunk, chunk)
+        rows = pl.ds(pl.multiple_of(row_first + first, chunk), chunk)
+        out_ref[pl.ds(first, chunk), :] = 0.5 * jnp.dot(
+            left[rows, :], right[...], preferred_element_type=jnp.float32
+        )
+
+
+def replicated(pair_blocks, dest_owner, dest_tile, chemical_potential):
+    col_count = lax.axis_size("col")
+    row_count = lax.axis_size("row")
+    depth_count = lax.axis_size("depth")
+    devices = row_count * col_count * depth_count
+    block_count = pair_blocks.shape[0]
+    grid_tiles = TC * col_count
+    order = grid_tiles * TILE
+    tile_rows = grid_tiles // row_count
+    labels = jnp.zeros((LABEL_ROWS, TILE), jnp.bfloat16)
+    labels = labels.at[0, :block_count].set(dest_tile.astype(jnp.bfloat16))
+    labels = labels.at[1, :block_count].set(dest_owner[:, 0].astype(jnp.bfloat16))
+    piece = jnp.concatenate([pair_blocks.reshape(block_count * TILE, TILE), labels], axis=0)
+    pieces = gather_pieces(piece, devices)
+    got = pieces[:, block_count * TILE : block_count * TILE + 2, :block_count].astype(jnp.int32)
+    row_of = jnp.arange(devices, dtype=jnp.int32)[:, None] // (col_count * depth_count)
+    tile_row = row_of * tile_rows + got[:, 0] // TC
+    tile_col = got[:, 1] * TC + got[:, 0] % TC
+    tiles = (tile_row * grid_tiles + tile_col).reshape(-1)
+    total = devices * block_count
+    index = jnp.arange(total, dtype=jnp.int32)
+    same = tiles[:, None] == tiles[None, :]
+    later = jnp.where(same & (index[None, :] > index[:, None]), index[None, :], total)
+    follower = jnp.min(later, axis=1)
+    follower = jnp.where(follower == total, -1, follower)
+    opened = jnp.any(same & (index[None, :] < index[:, None]), axis=1)
+    where = jnp.where(opened, -1, tiles)
+    place = jnp.stack([lax.axis_index("row"), lax.axis_index("col")]).astype(jnp.int32)
+    smem = pl.BlockSpec(memory_space=pltpu.SMEM)
+    return pl.pallas_call(
+        functools.partial(step_kernel, block_count, 512),
+        out_shape=jax.ShapeDtypeStruct((order // row_count, order // col_count), jnp.float32),
+        in_specs=[smem, smem, smem, smem, pl.BlockSpec(memory_space=pl.ANY)],
+        out_specs=pl.BlockSpec(memory_space=pltpu.VMEM),
+        scratch_shapes=[
+            pltpu.VMEM((devices, block_count * TILE, TILE), jnp.bfloat16),
+            pltpu.VMEM((order, order), jnp.bfloat16),
+            pltpu.VMEM((order, order // col_count), jnp.bfloat16),
+            pltpu.SemaphoreType.DMA(()),
+        ],
+        compiler_params=pltpu.CompilerParams(vmem_limit_bytes=60 * 2**20),
+    )(where, follower, place, chemical_potential, pieces)
+
+
 def solution(mesh):
     in_specs = (
         P(("row", "col", "depth"), None, None),
@@ -88,4 +351,7 @@
         P(),
     )
     out_specs = P("row", "col")
-    return jax.shard_map(shards, mesh=mesh, in_specs=in_specs, out_specs=out_specs, check_vma=False)
+    sizes = mesh.shape
+    small = sizes["row"] == 2 and sizes["depth"] == 2 and sizes["col"] == 8
+    body = replicated if small else shards
+    return jax.shard_map(body, mesh=mesh, in_specs=in_specs, out_specs=out_specs, check_vma=False)

time: 518 us -> 125 us (0.24)
  waiting for transfers between devices: 430 us -> 0 us
  Pallas kernels: 0 us -> 118 us
  local copies, waits for them, and re-layouts: 25.6 us -> 0.55 us
  matrix products: 21.7 us -> 0 us
  between operations: 14.2 us -> 0.7 us
  starting transfers between devices: 10.9 us -> 0 us
  other arithmetic: 14 us -> 5.87 us
    all_gather x5 -> x0, waiting for transfers between devices: 307 us -> none  [the longest x2 112 us: product(): return lax.all_gather(partial_rows, 'depth', axis=0, tiled=True)]
    pallas_call x0 -> x2, Pallas kernels: none -> 118 us  [the longest x1 69 us: gather_pieces(): pl.pallas_call(functools.partial(gather_kernel, z_count, (rows // 32 + 1)...]
    psum x1 -> x0, waiting for transfers between devices: 106 us -> none  [shards(): assembled = lax.psum(own_tiles, 'depth')]
    dot_general x4 -> x0, matrix products: 21.7 us -> none  [the longest x2 20.7 us: product(): jnp.dot(lax.all_gather(own_part, 'col', axis=1, tiled=True), row_panel, p...]
    all_to_all x2 -> x0, waiting for transfers between devices: 16.5 us -> none  [the longest x1 14.4 us: shards(): lax.all_to_all(send_blocks, 'col', split_axis=0, concat_axis=0, tiled=True)]
    reshape x4 -> x0, local copies, waits for them, and re-layouts: 12.2 us -> none  [the longest x1 5.45 us: shards(): assembled.reshape(tile_rows, TC, tile_size, tile_size).transpose(0, 2, 1, 3)]
    all_to_all x2 -> x0, starting transfers between devices: 10.5 us -> none  [the longest x1 6.38 us: shards(): lax.all_to_all(send_labels, 'col', split_axis=0, concat_axis=0, tiled=True)]
    unnamed x4 -> x0, local copies, waits for them, and re-layouts: 10.3 us -> none
  transfers between devices with their start and end apart: 8 -> 0, of which waited for: 8 -> 0; matrix products, arithmetic and copies ran while one was open for 1% -> 0% of each run, Pallas kernels for 0% -> 0%
where the time goes in v1:
time: 125 us
  Pallas kernels  118 us (94%)
  other arithmetic  5.87 us (5%)
    pallas_call x1, Pallas kernels, gather_pieces(): pl.pallas_call(functools.partial(gather_kernel, z_count, (rows // 32 + 1)...  69 us
    pallas_call x1, Pallas kernels, replicated(): pl.pallas_call(functools.partial(step_kernel, block_count, 512), out_shap...  48.6 us

profile of v1, /device:TPU:1, one launch (start us, length us, event | category | flops | bytes accessed | tf_op | source)
XLA Modules:
  0.0 124.7 jit_solution(10065487503743169473)
XLA Ops:
  0.7 0.7 pad_add_fusion.place_ref
  1.3 0.7 convert_bitcast_fusion
  2.0 0.7 convert_bitcast_fusion.1
  2.6 0.2 scatter.9
  2.8 0.1 add.80
  2.9 0.1 add.81
  3.0 1.8 %pad_maximum_fusion.own_ref = bf16[1680,128]{1,0:T(8,128)(2,1)} fusion(bf16[16,128]{1,0:T(8,128)(2,1)S(1)} %scatter.9, bf16[1664,128]{1,0:T(8,128)(2,1)} %bitcast.7), kind=kLoop, calls=%fused_computation.6 | loop fusion | flops 860160 | bytes 860160 | tf_op jit(solution)/shard_map/concatenate | solution.py:314
  4.8 69.0 %shard_map.46.all_ref = bf16[32,1680,128]{2,1,0:T(8,128)(2,1)} custom-call(bf16[1680,128]{1,0:T(8,128)(2,1)} %pad_maximum_fusion.own_ref), custom_call_target="tpu_custom_call" | custom-call | tf_op jit(solution)/shard_map/pallas_call | solution.py:204
  73.8 0.9 slice_convert_fusion
  74.7 0.1 slice_reduce_fusion
  74.8 0.1 squeeze.2
  74.9 0.1 mul.44
  75.0 0.2 fusion
  75.3 0.3 select_reduce_fusion
  75.6 0.6 compare_select_fusion
  76.2 48.6 %shard_map.47 = f32[2048,512]{1,0:T(8,128)} custom-call(s32[416]{0:T(512)} %get-tuple-element.32.where_ref, s32[416]{0:T(512)} %get-tuple-element.31.next_ref, s32[2]{0:T(128)} %pad_add_fusion.place_ref, f32[1]{0:T(128)S(6)} %copy.6.shift_ref, bf16[32,1680,128]{2,1,0:T(8,128)(2,1)} %shard_map.46.all_ref), custom_call_target="tpu_custom_call" | custom-call | tf_op jit(solution)/shard_map/pallas_call | solution.py:331
  (3 shorter events, 0.0 us)

commit v2 on v1

v2 whole, which is shorter than its diff:
```python
import functools

import jax
import jax.numpy as jnp
from jax import lax
from jax.experimental import pallas as pl
from jax.experimental.pallas import tpu as pltpu
from jax.sharding import PartitionSpec as P

TC = 4
CAP = 2
TILE = 128
LABEL_ROWS = 16


def assemble(received, labels, tile_count):
    one_hot = (
        labels.astype(jnp.float32)[None, :] == jnp.arange(tile_count, dtype=jnp.float32)[:, None]
    ).astype(jnp.bfloat16)
    return jnp.dot(one_hot, received, preferred_element_type=jnp.float32)


def product(left_matrix, right_matrix):
    layer_count = lax.axis_size("depth")
    layer_index = lax.axis_index("depth")
    rows_local, cols_local = left_matrix.shape
    half_rows = rows_local // layer_count
    own_part = lax.dynamic_slice_in_dim(left_matrix, layer_index * half_rows, half_rows, 0)
    row_panel = lax.all_gather(right_matrix, "row", axis=0, tiled=True)
    partial_rows = jnp.dot(
        lax.all_gather(own_part, "col", axis=1, tiled=True),
        row_panel,
        preferred_element_type=jnp.float32,
    )
    return lax.all_gather(partial_rows, "depth", axis=0, tiled=True)


def shards(pair_blocks, dest_owner, dest_tile, chemical_potential):
    col_count = lax.axis_size("col")
    row_count = lax.axis_size("row")
    block_count = pair_blocks.shape[0]
    tile_size = pair_blocks.shape[1]
    tile_rows = TC * col_count // row_count
    tile_count = tile_rows * TC
    flat_blocks = pair_blocks.reshape(block_count, tile_size * tile_size)
    owners = dest_owner[:, 0]
    owner_hot = (owners[:, None] == jnp.arange(col_count, dtype=jnp.int32)[None, :]).astype(
        jnp.int32
    )
    earlier = jnp.cumsum(owner_hot, axis=0) - owner_hot
    slot_rank = jnp.sum(earlier * owner_hot, axis=1)
    slot_index = owners * CAP + slot_rank
    picker = (slot_index[None, :] == jnp.arange(col_count * CAP, dtype=jnp.int32)[:, None]).astype(
        jnp.int32
    )
    send_blocks = jnp.dot(
        picker.astype(jnp.bfloat16), flat_blocks, preferred_element_type=jnp.float32
    ).astype(jnp.bfloat16)
    send_blocks = send_blocks.reshape(col_count, CAP, tile_size * tile_size)
    send_labels = (
        (jnp.sum(picker * (dest_tile[None, :] + 1), axis=1) - 1)
        .astype(jnp.float32)
        .astype(jnp.bfloat16)
    )
    send_labels = send_labels.reshape(col_count, CAP)
    got_blocks, got_labels = (
        lax.all_to_all(send_blocks, "col", split_axis=0, concat_axis=0, tiled=True),
        lax.all_to_all(send_labels, "col", split_axis=0, concat_axis=0, tiled=True),
    )
    own_tiles = assemble(
        got_blocks.reshape(-1, tile_size * tile_size), got_labels.reshape(-1), tile_count
    )
    assembled = lax.psum(own_tiles, "depth")
    hamiltonian = assembled.reshape(tile_rows, TC, tile_size, tile_size).transpose(0, 2, 1, 3)
    hamiltonian = hamiltonian.reshape(tile_rows * tile_size, TC * tile_size)
    rows_local, cols_local = hamiltonian.shape
    row_first = lax.axis_index("row") * rows_local
    col_first = lax.axis_index("col") * cols_local
    identity = (
        (row_first + jnp.arange(rows_local, dtype=jnp.int32))[:, None]
        == (col_first + jnp.arange(cols_local, dtype=jnp.int32))[None, :]
    ).astype(jnp.float32)
    left_matrix = (hamiltonian - chemical_potential[0] * identity).astype(jnp.bfloat16)
    squared = product(left_matrix, left_matrix)
    right_matrix = (3.0 * identity - squared).astype(jnp.bfloat16)
    return 0.5 * product(left_matrix, right_matrix)


def gather_kernel(spans, own_ref, all_ref, local_sem, send_sem, recv_sem):
    x = lax.axis_index("row")
    y = lax.axis_index("depth")
    c = lax.axis_index("col")
    z, q = c // 2, c % 2
    near = z + 1 - 2 * (z % 2)
    mid = (z + 2) % 4
    far = 3 - z
    inner = jnp.logical_or(z == 1, z == 2)

    def device(px, py, pz, pq):
        return {"row": px, "col": pz * 2 + pq, "depth": py}

    def chip(px, py, pz):
        return (px * 2 + py) * 4 + pz

    x_peer = device(1 - x, y, z, q)
    y_peer = device(x, 1 - y, z, q)
    sibling = device(x, y, z, 1 - q)
    near_peer, mid_peer, far_peer = (device(x, y, pz, q) for pz in (near, mid, far))
    peers = [near_peer, mid_peer, far_peer, x_peer, y_peer, sibling]

    barrier = pltpu.get_barrier_semaphore()
    for peer in peers:
        pl.semaphore_signal(barrier, inc=1, device_id=peer, device_id_type=pl.DeviceIdType.MESH)
    pl.semaphore_wait(barrier, len(peers))

    always, sometimes = [], []
    own = (x, y, z)

    def place(source, part, parity):
        px, py, pz = source
        first, size = spans[part]
        return all_ref.at[px * 16 + (pz * 2 + parity) * 2 + py, pl.ds(first, size)]

    def remote(source, part, peer, to_sibling=0):
        first, size = spans[part]
        return pltpu.make_async_remote_copy(
            src_ref=own_ref.at[pl.ds(first, size)] if source is own else place(source, part, q),
            dst_ref=place(source, part, q),
            send_sem=send_sem.at[len(always) + len(sometimes)],
            recv_sem=recv_sem.at[part, to_sibling, chip(*source)],
            device_id=peer,
            device_id_type=pl.DeviceIdType.MESH,
        )

    def send(source, part, peer, to_sibling=0):
        copy = remote(source, part, peer, to_sibling)
        copy.start()
        always.append(copy)

    def send_inner(source, part, peer):
        copy = remote(source, part, peer)
        sometimes.append(copy)

        @pl.when(inner)
        def _():
            copy.start()

    def share(source, part):
        send(source, part, sibling, 1)

    def arrived(source, part, from_sibling=0):
        target = place(source, part, 1 - q if from_sibling else q)
        pltpu.make_async_remote_copy(
            src_ref=target,
            dst_ref=target,
            send_sem=send_sem.at[0],
            recv_sem=recv_sem.at[part, from_sibling, chip(*source)],
            device_id=sibling,
            device_id_type=pl.DeviceIdType.MESH,
        ).wait_recv()

    first_peer, last_peer = (x_peer, y_peer), (y_peer, x_peer)

    def over_first(part, pz):
        return (1 - x, y, pz) if part == 0 else (x, 1 - y, pz)

    def over_last(part, pz):
        return (x, 1 - y, pz) if part == 0 else (1 - x, y, pz)

    def along_z(source):
        send(source, 2, near_peer)
        send(source, 2, mid_peer)
        send_inner(source, 2, far_peer)

    for part in range(2):
        send(own, part, mid_peer)
        send(own, part, near_peer)
        send_inner(own, part, far_peer)
    for part in range(2):
        send(own, part, first_peer[part])
    send(own, 2, x_peer)
    send(own, 2, y_peer)
    for part in range(2):
        send(own, part, last_peer[part])
    for part in range(3):
        share(own, part)
    keep = pltpu.make_async_copy(own_ref, all_ref.at[x * 16 + c * 2 + y], local_sem)
    keep.start()

    flats = [own, (1 - x, y, z), (x, 1 - y, z), (1 - x, 1 - y, z)]
    for step, pz in enumerate((z, near, mid, far)):
        for part in range(2):
            if step:
                source = (x, y, pz)
                arrived(source, part)
                if step == 2:
                    send_inner(source, part, near_peer)
                send(source, part, first_peer[part])
                send(source, part, last_peer[part])
                share(source, part)
        if step:
            flat = flats[step]
            arrived(flat, 2)
            if step == 1:
                send(flat, 2, y_peer)
                along_z(own)
            share(flat, 2)
            along_z(flat)
        for part in range(2):
            source = over_first(part, pz)
            arrived(source, part)
            send(source, part, last_peer[part])
            share(source, part)
    for step, pz in enumerate((z, mid, near, far)):
        if step:
            for px, py, _ in flats:
                source = (px, py, pz)
                arrived(source, 2)
                if step == 1:
                    send_inner(source, 2, near_peer)
                share(source, 2)
        for part in range(2):
            for source in (over_last(part, pz), (1 - x, 1 - y, pz)):
                arrived(source, part)
                share(source, part)
    for px in range(2):
        for py in range(2):
            for pz in range(4):
                for part in range(3):
                    arrived((px, py, pz), part, 1)
    for copy in always:
        copy.wait_send()
    for copy in sometimes:

        @pl.when(inner)
        def _():
            copy.wait_send()

    keep.wait()


def gather_pieces(piece, devices):
    rows, width = piece.shape
    units = rows // 16
    ends = [0, 40 * units // 105 * 16, 82 * units // 105 * 16, rows]
    spans = [(start, end - start) for start, end in zip(ends, ends[1:])]
    return pl.pallas_call(
        functools.partial(gather_kernel, spans),
        out_shape=jax.ShapeDtypeStruct((devices, rows, width), piece.dtype),
        in_specs=[pl.BlockSpec(memory_space=pl.ANY)],
        out_specs=pl.BlockSpec(memory_space=pl.ANY),
        scratch_shapes=[
            pltpu.SemaphoreType.DMA(()),
            pltpu.SemaphoreType.DMA((99,)),
            pltpu.SemaphoreType.DMA((3, 2, 16)),
        ],
        compiler_params=pltpu.CompilerParams(collective_id=0, has_side_effects=True),
    )(piece)


def step_kernel(
    block_count, chunk, row_ref, col_ref, follower_ref, chain_ref, place_ref, shift_ref, all_ref,
    out_ref, blocks, left, right, result, fetch_sem, store_sem
):
    devices = all_ref.shape[0]
    order = left.shape[0]
    grid_tiles = order // TILE
    rows_local, cols_local = out_ref.shape
    fetches = fetch_sem.shape[0]
    group = devices // fetches
    stores = store_sem.shape[0]
    slab = rows_local // stores
    shift = shift_ref[0]

    def fetch(h):
        part = pl.ds(h * group, group)
        return pltpu.make_async_copy(
            all_ref.at[part, pl.ds(0, block_count * TILE)], blocks.at[part], fetch_sem.at[h]
        )

    for h in range(fetches):
        fetch(h).start()

    eye = (
        lax.broadcasted_iota(jnp.int32, (TILE, TILE), 0)
        == lax.broadcasted_iota(jnp.int32, (TILE, TILE), 1)
    )
    shifted = jnp.where(eye, shift, 0.0)

    @pl.loop(0, grid_tiles)
    def _(i):
        rows = pl.ds(pl.multiple_of(i * TILE, TILE), TILE)
        left[rows, :] = jnp.zeros((TILE, order), left.dtype)
        left[rows, rows] = (-shifted).astype(left.dtype)

    def tile_of(b):
        return (
            pl.ds(pl.multiple_of(row_ref[b] * TILE, TILE), TILE),
            pl.ds(pl.multiple_of(col_ref[b] * TILE, TILE), TILE),
        )

    for h in range(fetches):
        fetch(h).wait()

        @pl.loop(h * group, (h + 1) * group)
        def _(g):
            for p in range(block_count):
                rows, cols = tile_of(g * block_count + p)
                left[rows, cols] = blocks[g, pl.ds(p * TILE, TILE), :]

    def block_of(b):
        row = pl.multiple_of((b % block_count) * TILE, TILE)
        return blocks[b // block_count, pl.ds(row, TILE), :].astype(jnp.float32)

    def write_sum(b):
        def add(carry):
            n, total = carry
            return follower_ref[n], total + block_of(n)

        _, total = lax.while_loop(
            lambda carry: carry[0] >= 0, add, (follower_ref[b], block_of(b))
        )
        rows, cols = tile_of(b)
        on_diagonal = row_ref[b] == col_ref[b]
        left[rows, cols] = (total - jnp.where(on_diagonal, shifted, 0.0)).astype(left.dtype)
        return chain_ref[b]

    lax.while_loop(lambda b: b < devices * block_count, write_sum, place_ref[2])

    row_first = place_ref[0] * rows_local
    col_first = pl.multiple_of(place_ref[1] * cols_local, cols_local)
    columns = pl.ds(col_first, cols_local)

    @pl.loop(0, order // chunk)
    def _(m):
        first = pl.multiple_of(m * chunk, chunk)
        rows = pl.ds(first, chunk)
        squared = jnp.dot(left[rows, :], left[:, columns], preferred_element_type=jnp.float32)
        on_diagonal = (
            first + lax.broadcasted_iota(jnp.int32, (chunk, cols_local), 0)
            == col_first + lax.broadcasted_iota(jnp.int32, (chunk, cols_local), 1)
        )
        right[rows, :] = (jnp.where(on_diagonal, 3.0, 0.0) - squared).astype(right.dtype)

    def store(m):
        part = pl.ds(m * slab, slab)
        return pltpu.make_async_copy(result.at[part], out_ref.at[part], store_sem.at[m])

    for m in range(stores):
        rows = pl.ds(pl.multiple_of(row_first + m * slab, slab), slab)
        result[pl.ds(m * slab, slab), :] = 0.5 * jnp.dot(
            left[rows, :], right[...], preferred_element_type=jnp.float32
        )
        store(m).start()
    for m in range(stores):
        store(m).wait()


def replicated(pair_blocks, dest_owner, dest_tile, chemical_potential):
    col_count = lax.axis_size("col")
    row_count = lax.axis_size("row")
    depth_count = lax.axis_size("depth")
    devices = row_count * col_count * depth_count
    block_count = pair_blocks.shape[0]
    grid_tiles = TC * col_count
    tile_rows = grid_tiles // row_count
    labels = jnp.zeros((LABEL_ROWS, TILE), jnp.bfloat16)
    labels = labels.at[0, :block_count].set(dest_tile.astype(jnp.bfloat16))
    labels = labels.at[1, :block_count].set(dest_owner[:, 0].astype(jnp.bfloat16))
    piece = jnp.concatenate([pair_blocks.reshape(block_count * TILE, TILE), labels], axis=0)
    pieces = gather_pieces(piece, devices)
    got = pieces[:, block_count * TILE : block_count * TILE + 2, :block_count].astype(jnp.int32)
    row_of = jnp.arange(devices, dtype=jnp.int32)[:, None] // (col_count * depth_count)
    tile_row = row_of * tile_rows + got[:, 0] // TC
    tile_col = got[:, 1] * TC + got[:, 0] % TC
    tile_row, tile_col = tile_row.reshape(-1), tile_col.reshape(-1)
    tiles = tile_row * grid_tiles + tile_col
    total = devices * block_count
    index = jnp.arange(total, dtype=jnp.int32)
    same = tiles[:, None] == tiles[None, :]
    follower = jnp.min(
        jnp.where(same & (index[None, :] > index[:, None]), index[None, :], total), axis=1
    )
    opens = ~jnp.any(same & (index[None, :] < index[:, None]), axis=1)
    special = opens & ((follower < total) | (tile_row == tile_col))
    follower = jnp.where(follower == total, -1, follower)
    chain = jnp.min(
        jnp.where(special[None, :] & (index[None, :] > index[:, None]), index[None, :], total),
        axis=1,
    )
    first = jnp.min(jnp.where(special, index, total))
    place = jnp.stack([lax.axis_index("row"), lax.axis_index("col"), first]).astype(jnp.int32)
    return step_call(
        (tile_row, tile_col, follower, chain, place, chemical_potential, pieces),
        block_count, 1024, row_count, col_count
    )


def step_call(operands, block_count, chunk, row_count, col_count):
    devices = operands[-1].shape[0]
    order = TC * col_count * TILE
    smem = pl.BlockSpec(memory_space=pltpu.SMEM)
    return pl.pallas_call(
        functools.partial(step_kernel, block_count, chunk),
        out_shape=jax.ShapeDtypeStruct((order // row_count, order // col_count), jnp.float32),
        in_specs=[smem] * 6 + [pl.BlockSpec(memory_space=pl.ANY)],
        out_specs=pl.BlockSpec(memory_space=pl.ANY),
        scratch_shapes=[
            pltpu.VMEM((devices, block_count * TILE, TILE), jnp.bfloat16),
            pltpu.VMEM((order, order), jnp.bfloat16),
            pltpu.VMEM((order, order // col_count), jnp.bfloat16),
            pltpu.VMEM((order // row_count, order // col_count), jnp.float32),
            pltpu.SemaphoreType.DMA((8,)),
            pltpu.SemaphoreType.DMA((4,)),
        ],
        compiler_params=pltpu.CompilerParams(vmem_limit_bytes=60 * 2**20),
    )(*operands)


def solution(mesh):
    in_specs = (
        P(("row", "col", "depth"), None, None),
        P(("row", "col", "depth"), None),
        P(("row", "col", "depth")),
        P(),
    )
    out_specs = P("row", "col")
    sizes = mesh.shape
    small = sizes["row"] == 2 and sizes["depth"] == 2 and sizes["col"] == 8
    body = replicated if small else shards
    return jax.shard_map(body, mesh=mesh, in_specs=in_specs, out_specs=out_specs, check_vma=False)
```

time: 125 us -> 112 us (0.90)
  Pallas kernels: 118 us -> 103 us
  other arithmetic: 5.87 us -> 7.85 us
    pallas_call x2, Pallas kernels: 118 us -> 103 us  [the longest x1 63 us: gather_pieces(): pl.pallas_call(functools.partial(gather_kernel, spans), out_shape=jax.Sha...]
    reduce_min x1 -> x3, other arithmetic: 0.33 us -> 2.3 us  [the longest x1 1.23 us: replicated(): first = jnp.min(jnp.where(special, index, total))]
where the time goes in v2:
time: 112 us
  Pallas kernels  103 us (92%)
  other arithmetic  7.85 us (7%)
    pallas_call x1, Pallas kernels, gather_pieces(): pl.pallas_call(functools.partial(gather_kernel, spans), out_shape=jax.Sha...  63 us
    pallas_call x1, Pallas kernels, step_call(): pl.pallas_call(functools.partial(step_kernel, block_count, chunk), out_sh...  39.8 us

profile of v2, /device:TPU:1, one launch (start us, length us, event | category | flops | bytes accessed | tf_op | source)
XLA Modules:
  0.0 112.1 jit_solution(8506974636085847913)
XLA Ops:
  0.7 0.7 convert_bitcast_fusion
  1.3 0.7 convert_bitcast_fusion.1
  2.0 0.2 scatter.9
  2.2 0.1 add.112
  2.2 0.1 add.113
  2.3 0.1 iota.41
  2.4 1.8 %pad_maximum_fusion.own_ref = bf16[1680,128]{1,0:T(8,128)(2,1)} fusion(bf16[16,128]{1,0:T(8,128)(2,1)S(1)} %scatter.9, bf16[1664,128]{1,0:T(8,128)(2,1)} %bitcast.8), kind=kLoop, calls=%fused_computation.8 | loop fusion | flops 860160 | bytes 860160 | tf_op jit(solution)/shard_map/concatenate | solution.py:370
  4.2 63.0 %shard_map.46.all_ref = bf16[32,1680,128]{2,1,0:T(8,128)(2,1)} custom-call(bf16[1680,128]{1,0:T(8,128)(2,1)} %pad_maximum_fusion.own_ref), custom_call_target="tpu_custom_call" | custom-call | tf_op jit(solution)/shard_map/pallas_call | solution.py:247
  67.3 0.9 slice_convert_fusion
  68.1 0.1 fusion.2
  68.2 0.1 mul.48
  68.3 0.1 squeeze.2
  68.5 0.0 copy-start
  68.5 0.0 copy-start.1
  68.5 0.2 fusion.1
  68.7 0.3 select_reduce_fusion.1
  69.0 1.2 %select_reduce_fusion.2 = (s32[]{:T(128)}, pred[416]{0:T(512)(128)(4,1)S(1)}, s32[416]{0:T(512)}) fusion(s32[416]{0:T(512)S(1)} %iota.41, s32[416]{0:T(512)S(1)} %get-tuple-element.35.row_ref, s32[416]{0:T(512)S(1)} %get-tuple-element.34.col_ref, s32[416]{0:T(512)S(1)} %select_reduce_fusion.1, pred[416]{0:T(512)(128)(4,1)S(1)} %fusion.1), kind=kLoop, calls=%fused_computation.22 | loop fusion | flops 3743 | bytes 9156 | tf_op jit(solution)/shard_map/reduce_min | solution.py:391
  70.3 1.2 %pad_add_fusion.place_ref = s32[3]{0:T(128)} fusion(s32[1]{0:T(128)} %bitcast.5, s32[1]{0:T(128)} %bitcast.4, s32[1]{0:T(128)} %bitcast.3), kind=kLoop, calls=%fused_computation.33 | loop fusion | flops 6 | bytes 24 | tf_op jit(solution)/shard_map/stack | solution.py:392
  71.5 0.7 select_reduce_fusion.chain_ref
  72.2 0.0 copy-done
  72.3 0.0 copy-done.1
  72.3 39.8 %shard_map.47 = f32[2048,512]{1,0:T(8,128)} custom-call(s32[416]{0:T(512)} %copy-done.1, s32[416]{0:T(512)} %copy-done, s32[416]{0:T(512)} %get-tuple-element.36.follower_ref, s32[416]{0:T(512)} %select_reduce_fusion.chain_ref, s32[3]{0:T(128)} %pad_add_fusion.place_ref, f32[1]{0:T(128)S(6)} %copy.6.shift_ref, bf16[32,1680,128]{2,1,0:T(8,128)(2,1)} %shard_map.46.all_ref), custom_call_target="tpu_custom_call" | custom-call | tf_op jit(solution)/shard_map/pallas_call | solution.py:403
  (4 shorter events, 0.0 us)
Async XLA Ops:
  68.5 3.8 %copy-start = (s32[416]{0:T(512)}, s32[416]{0:T(512)S(1)}, u32[]{:S(2)}) copy-start(s32[416]{0:T(512)S(1)} %get-tuple-element.34.col_ref) | copy-start | bytes 4996
  68.5 3.8 %copy-start.1 = (s32[416]{0:T(512)}, s32[416]{0:T(512)S(1)}, u32[]{:S(2)}) copy-start(s32[416]{0:T(512)S(1)} %get-tuple-element.35.row_ref) | copy-start | bytes 4996
